TPU v7x, 256 devices: a whole 4x4x8 slice. The times are simulated.
256 devices in a mesh: dp: 16 (over y_lo, x, core), chan: 16 (over y_hi, z).
Axes of the slice: x: 4, y: 4 (y_hi: 2, y_lo: 2; y = y_hi * 2 + y_lo), z: 8, core: 2. Of those that a mesh axis runs over, the one named last changes fastest.
Arguments:
- anchors: bfloat16 [256, 128, 4096], P('dp', 'chan'), may hold values from -15 to 15
- views: bfloat16 [256, 128, 4096], P('dp', 'chan'), may hold values from -15 to 15
- dw_weight: float32 [128, 4], replicated, may hold values from -3 to 3
- pw_weight: bfloat16 [256, 128], replicated, may hold values from -0.5 to 0.5
- proj_weight: bfloat16 [256, 1024], replicated, may hold values from -0.375 to 0.375
- partner: int32 [256], P('dp'), may hold values from 0 to 255, each once
Outputs:
- loss: float32 [256], P('dp')
- grad_dw: float32 [128, 4], P('chan')
- grad_pw: float32 [256, 128], replicated
- grad_proj: float32 [256, 1024], P('chan', 'dp')
Inputs may be any that keep to these rules, and one draw needn't show every extreme that they name: `partner`: each view index appears exactly once.
All inputs are finite; a program needn't handle non-finite values.
Results may differ from a plain program's by a relative error of at most 0.0044.
Values may be sent and summed in bfloat16 or wider, within the bound.
No kernel may reach another device: no remote copies, remote signals or barrier semaphores. Data moves between devices by JAX's collectives and lax.ppermute only.
A program may use at most 192 MiB of HBM per device.

v0:
```python
import jax
import jax.numpy as jnp
from jax import lax
from jax.sharding import PartitionSpec as P

TAPS = 4
TAP_SPACING = 16
logit_scale = 16.0


def passed_along(value, axis, steps):
    count = lax.axis_size(axis)
    pairs = [(source, (source + steps) % count) for source in range(count)]
    return lax.ppermute(value, axis, pairs)


def depthwise(trace_block, dw_weight):
    widened = trace_block.astype(jnp.float32)
    length = trace_block.shape[2]
    running = jnp.zeros(widened.shape, jnp.float32)
    for tap_index in range(TAPS):
        offset_steps = tap_index * TAP_SPACING
        shifted = jnp.pad(
            widened[:, :, : length - offset_steps], ((0, 0), (0, 0), (offset_steps, 0))
        )
        running = running + dw_weight[None, :, tap_index, None] * shifted
    return running.astype(jnp.bfloat16)


def silu_slope(mixed):
    sigma = jax.nn.sigmoid(mixed)
    return sigma * (1.0 + mixed * (1.0 - sigma))


def kernel_terms(grad_conv, extended):
    rim_width = (TAPS - 1) * TAP_SPACING
    span_width = grad_conv.shape[2]
    columns = []
    for tap_index in range(TAPS):
        begin = rim_width - tap_index * TAP_SPACING
        window = extended[:, :, begin : begin + span_width]
        columns.append(
            jnp.einsum("nct,nct->c", grad_conv, window, preferred_element_type=jnp.float32)
        )
    return jnp.stack(columns, 1)


def block_scores(queries, key_rows, owner_index, partner, factor):
    logits = factor * lax.dot_general(
        queries, key_rows, (((1,), (1,)), ((), ())), preferred_element_type=jnp.float32
    )
    columns = owner_index * key_rows.shape[0] + jnp.arange(key_rows.shape[0], dtype=jnp.int32)
    matches = columns[None, :] == partner[:, None]
    return (logits, matches)


def body(anchors, views, dw_weight, pw_weight, proj_weight, partner):
    stacked = jnp.concatenate([anchors, views], 0)
    pair_count = anchors.shape[0]
    length = anchors.shape[2]
    chan_index = lax.axis_index("chan")
    chan_count = lax.axis_size("chan")
    cycle_index = lax.axis_index("dp")
    cycle_size = lax.axis_size("dp")
    rim_width = (TAPS - 1) * TAP_SPACING
    local_metrics = anchors.shape[1]
    local_kernel = lax.dynamic_slice_in_dim(dw_weight, chan_index * local_metrics, local_metrics, 0)
    conv_local = depthwise(stacked, local_kernel)
    conv_rows = lax.all_to_all(conv_local, "chan", split_axis=2, concat_axis=1, tiled=True)
    mixed = jnp.einsum("fc,nct->nft", pw_weight, conv_rows, preferred_element_type=jnp.float32)
    partial_pool = jnp.sum(jax.nn.silu(mixed), 2) / length
    conv_time, mixed, partial_pool = (conv_rows, mixed, partial_pool)
    pooled = lax.psum(partial_pool, "chan")
    pooled_bf = pooled.astype(jnp.bfloat16)
    embedding = jnp.dot(pooled_bf, proj_weight, preferred_element_type=jnp.float32)
    inverse = lax.rsqrt(jnp.mean(embedding * embedding, 1, keepdims=True) + 1e-06)
    unit_rows = embedding * inverse
    unit_bf = unit_rows.astype(jnp.bfloat16)
    queries = unit_bf[:pair_count]
    own_keys = unit_bf[pair_count:]
    factor = logit_scale / proj_weight.shape[1]

    def total_terms(key_rows, owner_index, totals, positive):
        logits, matches = block_scores(queries, key_rows, owner_index, partner, factor)
        totals = totals + jnp.sum(jnp.exp(logits - logit_scale), 1)
        positive = positive + jnp.sum(jnp.where(matches, logits, 0.0), 1)
        return (totals, positive)

    def first_turn(turn_index, loop_state):
        key_rows, totals, positive = loop_state
        owner_index = (cycle_index - turn_index) % cycle_size
        totals, positive = total_terms(key_rows, owner_index, totals, positive)
        key_rows = passed_along(key_rows, "dp", 1)
        return (key_rows, totals, positive)

    start_zero = jnp.zeros((pair_count,), jnp.float32)
    key_rows, totals, positive = lax.fori_loop(
        0, cycle_size - 1, first_turn, (own_keys, start_zero, start_zero)
    )
    totals, positive = total_terms(
        key_rows, (cycle_index - (cycle_size - 1)) % cycle_size, totals, positive
    )

    def grad_terms(key_rows, owner_index, carried, grad_query):
        logits, matches = block_scores(queries, key_rows, owner_index, partner, factor)
        coeffs = (
            jnp.exp(logits - logit_scale) / totals[:, None] - matches.astype(jnp.float32)
        ).astype(jnp.bfloat16)
        grad_query = grad_query + factor * jnp.dot(
            coeffs, key_rows, preferred_element_type=jnp.float32
        )
        carried = carried + factor * lax.dot_general(
            coeffs, queries, (((0,), (0,)), ((), ())), preferred_element_type=jnp.float32
        )
        return (carried, grad_query)

    def second_turn(turn_index, loop_state):
        key_rows, carried, grad_query = loop_state
        owner_index = (cycle_index - turn_index) % cycle_size
        carried, grad_query = grad_terms(key_rows, owner_index, carried, grad_query)
        key_rows = passed_along(key_rows, "dp", 1)
        carried = passed_along(carried, "dp", 1)
        return (key_rows, carried, grad_query)

    start_grads = jnp.zeros(own_keys.shape, jnp.float32)
    key_rows, carried, grad_query = lax.fori_loop(
        0, cycle_size - 1, second_turn, (own_keys, start_grads, start_grads)
    )
    carried, grad_query = grad_terms(
        key_rows, (cycle_index - (cycle_size - 1)) % cycle_size, carried, grad_query
    )
    grad_key = passed_along(carried, "dp", 1)
    losses = logit_scale + jnp.log(totals) - positive
    grad_unit = jnp.concatenate([grad_query, grad_key], 0)
    grad_embed = inverse * (
        grad_unit - unit_rows * jnp.mean(unit_rows * grad_unit, 1, keepdims=True)
    )
    grad_embed_bf = grad_embed.astype(jnp.bfloat16)
    filter_rows = proj_weight.shape[0] // chan_count
    pooled_rows = lax.dynamic_slice_in_dim(pooled_bf, chan_index * filter_rows, filter_rows, 1)
    proj_terms = lax.dot_general(
        pooled_rows, grad_embed_bf, (((0,), (0,)), ((), ())), preferred_element_type=jnp.float32
    )
    grad_proj = lax.psum_scatter(proj_terms, "dp", scatter_dimension=1, tiled=True)
    grad_pool = lax.dot_general(
        grad_embed_bf, proj_weight, (((1,), (1,)), ((), ())), preferred_element_type=jnp.float32
    )
    grad_mixed = (grad_pool[:, :, None] / length * silu_slope(mixed)).astype(jnp.bfloat16)
    mix_terms = jnp.einsum("nft,nct->fc", grad_mixed, conv_time, preferred_element_type=jnp.float32)
    grad_conv = jnp.einsum(
        "fc,nft->nct", pw_weight, grad_mixed, preferred_element_type=jnp.float32
    ).astype(jnp.bfloat16)
    grad_pw = lax.psum(mix_terms, ("dp", "chan"))
    grad_local = lax.all_to_all(grad_conv, "chan", split_axis=1, concat_axis=2, tiled=True)
    extended = jnp.pad(stacked, ((0, 0), (0, 0), (rim_width, 0)))
    kernel_part = kernel_terms(grad_local, extended)
    grad_dw = lax.psum(kernel_part, "dp")
    return (losses, grad_dw, grad_pw, grad_proj)


def solution(mesh):
    placed = (P("dp", "chan", None), P("dp", "chan", None), P(), P(), P(), P("dp"))
    return jax.shard_map(
        body,
        mesh=mesh,
        in_specs=placed,
        out_specs=(P("dp"), P("chan", None), P(), P("chan", "dp")),
        check_vma=False,
    )
```

profile of v0, /device:TPU:2, one launch (start us, length us, event | category | flops | bytes accessed | tf_op | source)
XLA Modules:
  0.0 708.4 jit_solution(9025586352325555345)
XLA Ops:
  10.7 7.9 %copy.34 = bf16[32,8,4096]{0,1,2:T(8,128)(2,1)} copy(bf16[32,8,4096]{2,1,0:T(8,128)(2,1)S(1)} %constant_dynamic-update-slice_fusion) | data formatting | bytes 4194304 | tf_op jit(solution)/shard_map/concatenate | solution.py:58
  18.6 10.5 %slice.49 = f32[32,8,4080]{0,1,2:T(8,128)} slice(bf16[32,8,4096]{0,1,2:T(8,128)(2,1)} %copy.34), slice={[0:32], [0:8], [0:4080]} | slice | bytes 8355840 | tf_op jit(solution)/shard_map/slice | solution.py:24
  30.5 6.0 slice.50
  36.5 6.0 slice.51
  42.5 23.1 %fusion.44 = bf16[4096,8,32]{2,1,0:T(8,128)(2,1)} fusion(f32[32,8,4048]{0,1,2:T(8,128)} %slice.51, f32[8]{0:T(128)S(1)} %get-tuple-element.488, f32[32,8,4064]{0,1,2:T(8,128)} %slice.50, f32[8]{0:T(128)S(1)} %get-tuple-element.489, f32[32,8,4080]{0,1,2:T(8,128)} %slice.49, f32[8]{0:T(128)S(1)} %get-tuple-element.490, bf16[32,8,4096]{0,1,2:T(8,128)(2,1)} %copy.34, ...), kind=kLoop, calls=%fused_computation.88 | loop fusion | flops 9437184 | bytes 16679040
  65.6 14.5 %reshape.59 = bf16[16,2,32768]{2,1,0:T(2,128)(2,1)} reshape(bf16[4096,8,32]{2,1,0:T(8,128)(2,1)} %fusion.44) | data formatting | bytes 4194304
  80.1 11.3 %all-to-all-start = ((bf16[16,2,32768]{2,1,0:T(2,128)(2,1)}), bf16[16,2,32768]{2,1,0:T(2,128)(2,1)}, u32[]{:S(2)}, u32[]{:S(2)}) async-start(bf16[16,2,32768]{2,1,0:T(2,128)(2,1)} %reshape.59), calls=%async_computation | async-start | bytes 4194304 | tf_op jit(solution)/shard_map/all_to_all | solution.py:69
  91.4 50.5 %all-to-all-done = bf16[16,2,32768]{2,1,0:T(2,128)(2,1)} async-done(((bf16[16,2,32768]{2,1,0:T(2,128)(2,1)}), bf16[16,2,32768]{2,1,0:T(2,128)(2,1)}, u32[]{:S(2)}, u32[]{:S(2)}) %all-to-all-start) | async-done | bytes 2097184 | tf_op jit(solution)/shard_map/all_to_all | solution.py:69
  141.9 12.9 %reshape.60 = bf16[4096,8,32]{2,1,0:T(8,128)(2,1)} reshape(bf16[16,2,32768]{2,1,0:T(2,128)(2,1)} %all-to-all-done) | data formatting | bytes 4194304
  154.8 10.5 %copy.36 = bf16[32,16,8,256]{3,2,1,0:T(8,128)(2,1)} copy(bf16[32,16,8,256]{0,2,3,1:T(8,128)(2,1)} %bitcast.123) | data formatting | bytes 4194304 | tf_op jit(solution)/shard_map/all_to_all | solution.py:69
  165.3 6.2 fusion.12
  171.5 74.3 %psum.21 = bf16[32,256]{1,0:T(8,128)(2,1)S(1)} all-reduce(f32[32,256]{1,0:T(8,128)S(1)} %broadcast_multiply_fusion), channel_id=1, replica_groups=mesh['dp'=16,'chan'=16] {'chan'}, use_global_device_ids=true, to_apply=%region_1.2 | all-reduce | flops 8192 | bytes 49152 | tf_op jit(solution)/shard_map/psum | solution.py:73
  246.3 74.0 %while.40 = (s32[]{:T(128)}, bf16[16,1024]{1,0:T(8,128)(2,1)S(1)}, f32[16]{0:T(128)S(1)}, f32[16]{0:T(128)S(1)}, bf16[16,1024]{1,0:T(8,128)(2,1)S(1)}, /*index=5...) while((s32[]{:T(128)}, bf16[16,1024]{1,0:T(8,128)(2,1)S(1)}, ...), condition=%wide.region_6.7_spmd.clone, body=%wide.region_3.6_spmd.clone.sunk | while | flops 525888 | bytes 263144 | solution.py:97
  260.4 5.3 collective-permute-done
  265.9 5.3 collective-permute-done
  271.3 5.3 collective-permute-done
  282.2 5.3 collective-permute-done
  287.7 5.3 collective-permute-done
  293.2 5.3 collective-permute-done
  320.9 92.6 %while.41 = (s32[]{:T(128)}, bf16[16,1024]{1,0:T(8,128)(2,1)S(1)}, f32[16,1024]{1,0:T(8,128)S(1)}, f32[16,1024]{1,0:T(8,128)S(1)}, bf16[16,1024]{1,0:T(8,128)(2,...) while((s32[]{:T(128)}, bf16[16,1024]{1,0:T(8,128)(2,1)S(1)}, ...), condition=%wide.region_10.11_spmd.clone, body=%wide.region_9.10_spmd.clone.sunk | while | flops 1656608 | bytes 854104 | solution.py:126
  414.2 5.6 collective-permute-done.3
  445.1 64.7 %reduce-scatter.4.cloned.1.call-done = f32[64,16]{1,0:T(8,128)} async-done(((f32[1024,16]{1,0:T(8,128)}), f32[64,16]{1,0:T(8,128)}) %reduce-scatter.4.cloned.1.call-update) | async-done | bytes 4112
  516.8 28.9 %psum.22 = f32[8,4]{0,1:T(4,128)} all-reduce(f32[8,4]{0,1:T(4,128)S(1)} %pad_maximum_fusion.1), channel_id=1, replica_groups=mesh['dp'=16,'chan'=16] {'dp'}, use_global_device_ids=true, to_apply=%region_12.13 | all-reduce | flops 32 | bytes 256 | tf_op jit(solution)/shard_map/psum | solution.py:157
  545.7 153.7 %all-reduce.6.cloned.1.call-done = f32[256,128]{1,0:T(8,128)} async-done(((f32[256,128]{1,0:T(8,128)}), f32[256,128]{1,0:T(8,128)}) %all-reduce.6.cloned.1.call-update) | async-done | bytes 131088 | tf_op jit(solution)/shard_map/psum | solution.py:153
  (272 shorter events, 174.2 us)
Async XLA Ops:
  80.1 61.8 %all-to-all-start = ((bf16[16,2,32768]{2,1,0:T(2,128)(2,1)}), bf16[16,2,32768]{2,1,0:T(2,128)(2,1)}, u32[]{:S(2)}, u32[]{:S(2)}) async-start(bf16[16,2,32768]{2,1,0:T(2,128)(2,1)} %reshape.59), calls=%async_computation | async-start | bytes 4194304 | tf_op jit(solution)/shard_map/all_to_all | solution.py:69
  260.2 5.4 collective-permute-start
  265.7 5.4 collective-permute-start
  271.2 5.4 collective-permute-start
  320.9 5.5 collective-permute-start.1
  321.4 5.9 collective-permute-start.2
  327.6 5.6 collective-permute-start.2
  333.4 5.9 collective-permute-start.2
  339.6 5.9 collective-permute-start.2
  345.8 5.9 collective-permute-start.2
  352.0 5.9 collective-permute-start.2
  358.2 5.9 collective-permute-start.2
  364.4 5.9 collective-permute-start.2
  370.5 5.9 collective-permute-start.2
  376.7 5.9 collective-permute-start.2
  382.9 5.9 collective-permute-start.2
  389.1 5.9 collective-permute-start.2
  395.3 5.9 collective-permute-start.2
  401.5 5.9 collective-permute-start.2
  407.7 5.9 collective-permute-start.2
  413.8 6.1 collective-permute-start.3
  434.6 76.7 %all-to-all-start.1 = ((bf16[32,128,256]{2,0,1:T(8,128)(2,1)}), bf16[32,128,256]{2,0,1:T(8,128)(2,1)}, u32[]{:S(2)}, u32[]{:S(2)}) async-start(bf16[32,128,256]{2,0,1:T(8,128)(2,1)} %copy.39), calls=%async_computation.1 | async-start | bytes 4194304 | tf_op jit(solution)/shard_map/all_to_all | solution.py:154
  439.0 70.8 %reduce-scatter.4.cloned.1.call-start = ((), (), s32[]{:S(2)}) async-start(), calls=%async_computation.4 | async-start | bytes 557056
  440.2 259.2 %all-reduce.6.cloned.1.call-start = ((), (), s32[]{:S(2)}) async-start(), calls=%async_computation.3 | async-start | bytes 262144 | tf_op jit(solution)/shard_map/psum | solution.py:153
  (32 other events, 546.0 us)
Sparse Core Ops, SparseCore 0:
  442.3 67.4 reduce-scatter.3
Sparse Core Ops, SparseCore 1:
  446.8 252.6 all-reduce.5
where the time goes:
time: 710 us; the launch traced here: 708 us
  waiting for transfers between devices  403 us (57%)
  blocking collectives  103 us (15%)
  local copies, waits for them, and re-layouts  84.8 us (12%)
  starting transfers between devices  43.8 us (6%)
  other arithmetic  32.1 us (5%)
  matrix products  24.8 us (3%)
  between operations  15.7 us (2%)
    psum x1, waiting for transfers between devices, body(): grad_pw = lax.psum(mix_terms, ('dp', 'chan'))  154 us
    ppermute x46, waiting for transfers between devices, passed_along(): return lax.ppermute(value, axis, pairs)  135 us
    psum x1, blocking collectives, body(): pooled = lax.psum(partial_pool, 'chan')  74.3 us
    unnamed x3, waiting for transfers between devices  64.7 us
    all_to_all x1, waiting for transfers between devices, body(): lax.all_to_all(conv_local, 'chan', split_axis=2, concat_axis=1, tiled=True)  50.5 us
    unnamed x18, local copies, waits for them, and re-layouts  35.1 us
    psum x1, blocking collectives, body(): grad_dw = lax.psum(kernel_part, 'dp')  28.9 us
    ppermute x46, starting transfers between devices, passed_along(): return lax.ppermute(value, axis, pairs)  28.1 us
  transfers between devices with their start and end apart: 50, of which 49 were waited for; matrix products, arithmetic and copies ran while one was open for 3% of the time, Pallas kernels for 0%

commit v1 on v0

--- a/solution.py
+++ b/solution.py
@@ -6,6 +6,11 @@
 TAPS = 4
 TAP_SPACING = 16
 logit_scale = 16.0
+
+
+def one_after_other(value_2, axis_one, axis_two):
+    inner = lax.psum(value_2, axis_one)
+    return lax.psum(inner, axis_two)
 
 
 def passed_along(value, axis, steps):
@@ -150,7 +155,7 @@
     grad_conv = jnp.einsum(
         "fc,nft->nct", pw_weight, grad_mixed, preferred_element_type=jnp.float32
     ).astype(jnp.bfloat16)
-    grad_pw = lax.psum(mix_terms, ("dp", "chan"))
+    grad_pw = one_after_other(mix_terms, "chan", "dp")
     grad_local = lax.all_to_all(grad_conv, "chan", split_axis=1, concat_axis=2, tiled=True)
     extended = jnp.pad(stacked, ((0, 0), (0, 0), (rim_width, 0)))
     kernel_part = kernel_terms(grad_local, extended)

time: 710 us -> 739 us (1.041)
  waiting for transfers between devices: 403 us -> 433 us
    psum x1 -> x2, waiting for transfers between devices: 154 us -> 183 us  [the longest x1 98.1 us: one_after_other(): inner = lax.psum(value_2, axis_one)]
    unnamed x3 -> x4, waiting for transfers between devices: 64.7 us -> 65 us
  transfers between devices with their start and end apart: 50 -> 51, of which waited for: 49 -> 50; matrix products, arithmetic and copies ran while one was open for 3% -> 3% of each run, Pallas kernels for 0% -> 0%
where the time goes in v1:
time: 739 us; the launch traced here: 734 us
  waiting for transfers between devices  433 us (59%)
  blocking collectives  98.2 us (13%)
  local copies, waits for them, and re-layouts  84.8 us (11%)
  starting transfers between devices  43.9 us (6%)
  other arithmetic  32.1 us (4%)
  matrix products  24.8 us (3%)
  between operations  15.7 us (2%)
    ppermute x46, waiting for transfers between devices, passed_along(): return lax.ppermute(value, axis, pairs)  135 us
    psum x1, waiting for transfers between devices, one_after_other(): inner = lax.psum(value_2, axis_one)  98.1 us
    psum x1, waiting for transfers between devices, one_after_other(): return lax.psum(inner, axis_two)  85.4 us
    psum x1, blocking collectives, body(): pooled = lax.psum(partial_pool, 'chan')  74.3 us
    unnamed x4, waiting for transfers between devices  65 us
    all_to_all x1, waiting for transfers between devices, body(): lax.all_to_all(conv_local, 'chan', split_axis=2, concat_axis=1, tiled=True)  50.5 us
    unnamed x18, local copies, waits for them, and re-layouts  35.1 us
    ppermute x46, starting transfers between devices, passed_along(): return lax.ppermute(value, axis, pairs)  28.1 us
  transfers between devices with their start and end apart: 51, of which 50 were waited for; matrix products, arithmetic and copies ran while one was open for 3% of the time, Pallas kernels for 0%

profile of v1, /device:TPU:2, one launch (start us, length us, event | category | flops | bytes accessed | tf_op | source)
XLA Modules:
  0.0 733.5 jit_solution(12984944249497556484)
XLA Ops:
  10.7 7.9 %copy.34 = bf16[32,8,4096]{0,1,2:T(8,128)(2,1)} copy(bf16[32,8,4096]{2,1,0:T(8,128)(2,1)S(1)} %constant_dynamic-update-slice_fusion) | data formatting | bytes 4194304 | tf_op jit(solution)/shard_map/concatenate | solution.py:63
  18.6 10.5 %slice.49 = f32[32,8,4080]{0,1,2:T(8,128)} slice(bf16[32,8,4096]{0,1,2:T(8,128)(2,1)} %copy.34), slice={[0:32], [0:8], [0:4080]} | slice | bytes 8355840 | tf_op jit(solution)/shard_map/slice | solution.py:29
  30.5 6.0 slice.50
  36.5 6.0 slice.51
  42.5 23.1 %fusion.44 = bf16[4096,8,32]{2,1,0:T(8,128)(2,1)} fusion(f32[32,8,4048]{0,1,2:T(8,128)} %slice.51, f32[8]{0:T(128)S(1)} %get-tuple-element.488, f32[32,8,4064]{0,1,2:T(8,128)} %slice.50, f32[8]{0:T(128)S(1)} %get-tuple-element.489, f32[32,8,4080]{0,1,2:T(8,128)} %slice.49, f32[8]{0:T(128)S(1)} %get-tuple-element.490, bf16[32,8,4096]{0,1,2:T(8,128)(2,1)} %copy.34, ...), kind=kLoop, calls=%fused_computation.88 | loop fusion | flops 9437184 | bytes 16679040
  65.6 14.5 %reshape.59 = bf16[16,2,32768]{2,1,0:T(2,128)(2,1)} reshape(bf16[4096,8,32]{2,1,0:T(8,128)(2,1)} %fusion.44) | data formatting | bytes 4194304
  80.1 11.3 %all-to-all-start = ((bf16[16,2,32768]{2,1,0:T(2,128)(2,1)}), bf16[16,2,32768]{2,1,0:T(2,128)(2,1)}, u32[]{:S(2)}, u32[]{:S(2)}) async-start(bf16[16,2,32768]{2,1,0:T(2,128)(2,1)} %reshape.59), calls=%async_computation | async-start | bytes 4194304 | tf_op jit(solution)/shard_map/all_to_all | solution.py:74
  91.4 50.5 %all-to-all-done = bf16[16,2,32768]{2,1,0:T(2,128)(2,1)} async-done(((bf16[16,2,32768]{2,1,0:T(2,128)(2,1)}), bf16[16,2,32768]{2,1,0:T(2,128)(2,1)}, u32[]{:S(2)}, u32[]{:S(2)}) %all-to-all-start) | async-done | bytes 2097184 | tf_op jit(solution)/shard_map/all_to_all | solution.py:74
  141.9 12.9 %reshape.60 = bf16[4096,8,32]{2,1,0:T(8,128)(2,1)} reshape(bf16[16,2,32768]{2,1,0:T(2,128)(2,1)} %all-to-all-done) | data formatting | bytes 4194304
  154.8 10.5 %copy.36 = bf16[32,16,8,256]{3,2,1,0:T(8,128)(2,1)} copy(bf16[32,16,8,256]{0,2,3,1:T(8,128)(2,1)} %bitcast.123) | data formatting | bytes 4194304 | tf_op jit(solution)/shard_map/all_to_all | solution.py:74
  165.3 6.2 fusion.12
  171.5 74.3 %psum.28 = bf16[32,256]{1,0:T(8,128)(2,1)S(1)} all-reduce(f32[32,256]{1,0:T(8,128)S(1)} %broadcast_multiply_fusion), channel_id=1, replica_groups=mesh['dp'=16,'chan'=16] {'chan'}, use_global_device_ids=true, to_apply=%region_1.2 | all-reduce | flops 8192 | bytes 49152 | tf_op jit(solution)/shard_map/psum | solution.py:78
  246.3 74.0 %while.40 = (s32[]{:T(128)}, bf16[16,1024]{1,0:T(8,128)(2,1)S(1)}, f32[16]{0:T(128)S(1)}, f32[16]{0:T(128)S(1)}, bf16[16,1024]{1,0:T(8,128)(2,1)S(1)}, /*index=5...) while((s32[]{:T(128)}, bf16[16,1024]{1,0:T(8,128)(2,1)S(1)}, ...), condition=%wide.region_6.7_spmd.clone, body=%wide.region_3.6_spmd.clone.sunk | while | flops 525888 | bytes 263144 | solution.py:102
  260.4 5.3 collective-permute-done
  265.9 5.3 collective-permute-done
  271.3 5.3 collective-permute-done
  282.2 5.3 collective-permute-done
  287.7 5.3 collective-permute-done
  320.9 92.6 %while.41 = (s32[]{:T(128)}, bf16[16,1024]{1,0:T(8,128)(2,1)S(1)}, f32[16,1024]{1,0:T(8,128)S(1)}, f32[16,1024]{1,0:T(8,128)S(1)}, bf16[16,1024]{1,0:T(8,128)(2,...) while((s32[]{:T(128)}, bf16[16,1024]{1,0:T(8,128)(2,1)S(1)}, ...), condition=%wide.region_10.11_spmd.clone, body=%wide.region_9.10_spmd.clone.sunk | while | flops 1656608 | bytes 854104 | solution.py:131
  414.2 5.6 collective-permute-done.3
  445.1 64.9 %reduce-scatter.4.cloned.1.call-done = f32[64,16]{1,0:T(8,128)} async-done(((f32[1024,16]{1,0:T(8,128)}), f32[64,16]{1,0:T(8,128)}) %reduce-scatter.4.cloned.1.call-update) | async-done | bytes 4112
  511.5 98.1 %all-reduce.7.cloned.1.call-done = f32[256,128]{1,0:T(8,128)} async-done(((f32[256,128]{1,0:T(8,128)}), f32[256,128]{1,0:T(8,128)}) %all-reduce.7.cloned.1.call-update) | async-done | bytes 131088 | tf_op jit(solution)/shard_map/psum | solution.py:12
  615.2 23.9 %psum.29 = f32[8,4]{0,1:T(4,128)} all-reduce(f32[8,4]{0,1:T(4,128)S(1)} %pad_maximum_fusion.1), channel_id=1, replica_groups=mesh['dp'=16,'chan'=16] {'dp'}, use_global_device_ids=true, to_apply=%region_12.13 | all-reduce | flops 32 | bytes 256 | tf_op jit(solution)/shard_map/psum | solution.py:162
  639.1 85.4 %all-reduce.9.cloned.1.call-done = f32[256,128]{1,0:T(8,128)} async-done(((f32[256,128]{1,0:T(8,128)}), f32[256,128]{1,0:T(8,128)}) %all-reduce.9.cloned.1.call-update) | async-done | bytes 131088 | tf_op jit(solution)/shard_map/psum | solution.py:13
  (275 shorter events, 179.5 us)
Async XLA Ops:
  80.1 61.8 %all-to-all-start = ((bf16[16,2,32768]{2,1,0:T(2,128)(2,1)}), bf16[16,2,32768]{2,1,0:T(2,128)(2,1)}, u32[]{:S(2)}, u32[]{:S(2)}) async-start(bf16[16,2,32768]{2,1,0:T(2,128)(2,1)} %reshape.59), calls=%async_computation | async-start | bytes 4194304 | tf_op jit(solution)/shard_map/all_to_all | solution.py:74
  260.2 5.4 collective-permute-start
  265.7 5.4 collective-permute-start
  320.9 5.5 collective-permute-start.1
  321.4 5.9 collective-permute-start.2
  327.6 5.6 collective-permute-start.2
  333.4 5.9 collective-permute-start.2
  339.6 5.9 collective-permute-start.2
  345.8 5.9 collective-permute-start.2
  352.0 5.9 collective-permute-start.2
  358.2 5.9 collective-permute-start.2
  364.4 5.9 collective-permute-start.2
  370.5 5.9 collective-permute-start.2
  376.7 5.9 collective-permute-start.2
  382.9 5.9 collective-permute-start.2
  389.1 5.9 collective-permute-start.2
  395.3 5.9 collective-permute-start.2
  401.5 5.9 collective-permute-start.2
  407.7 5.9 collective-permute-start.2
  413.8 6.1 collective-permute-start.3
  434.6 175.1 %all-to-all-start.1 = ((bf16[32,128,256]{2,0,1:T(8,128)(2,1)}), bf16[32,128,256]{2,0,1:T(8,128)(2,1)}, u32[]{:S(2)}, u32[]{:S(2)}) async-start(bf16[32,128,256]{2,0,1:T(8,128)(2,1)} %copy.39), calls=%async_computation.1 | async-start | bytes 4194304 | tf_op jit(solution)/shard_map/all_to_all | solution.py:159
  439.0 71.1 %reduce-scatter.4.cloned.1.call-start = ((), (), s32[]{:S(2)}) async-start(), calls=%async_computation.5 | async-start | bytes 557056
  440.2 169.4 %all-reduce.7.cloned.1.call-start = ((), (), s32[]{:S(2)}) async-start(), calls=%async_computation.3 | async-start | bytes 262144 | tf_op jit(solution)/shard_map/psum | solution.py:12
  445.1 279.4 %all-reduce.9.cloned.1.call-start = ((), (), s32[]{:S(2)}) async-start(), calls=%async_computation.4 | async-start | bytes 262144 | tf_op jit(solution)/shard_map/psum | solution.py:13
  (33 other events, 551.4 us)
Sparse Core Ops, SparseCore 0:
  442.3 67.6 reduce-scatter.3
  609.7 114.7 all-reduce.8
Sparse Core Ops, SparseCore 1:
  445.2 164.4 all-reduce.6
